TPU v7x, 32 devices: a whole 2x2x4 slice. The times are simulated.
32 devices in a mesh: strip: 4 (over z), cross: 8 (over y, x, core).
Axes of the slice: x: 2, y: 2, z: 4, core: 2. Of those that a mesh axis runs over, the one named last changes fastest.
Arguments:
- rhs: bfloat16 [4, 64, 14336], P('strip', None, 'cross'), may hold values from -6 to 6
- inverse: bfloat16 [4, 8, 1792, 1792], P('strip', 'cross'), may hold values from -2 to 2
- dis_fwd: bfloat16 [4, 8, 256, 1792], P('strip', 'cross'), may hold values from -0.1875 to 0.1875
- agg_fwd: bfloat16 [4, 14336, 256], P('strip', 'cross'), may hold values from -0.0625 to 0.0625
- phase_fwd: float32 [4, 128], P('strip'), may hold values from -3.140625 to 3.140625
- gain_fwd: float32 [4, 128], P('strip'), may hold values from 0.5 to 1
- dis_back: bfloat16 [4, 8, 256, 1792], P('strip', 'cross'), may hold values from -0.1875 to 0.1875
- agg_back: bfloat16 [4, 14336, 256], P('strip', 'cross'), may hold values from -0.0625 to 0.0625
- phase_back: float32 [4, 128], P('strip'), may hold values from -3.140625 to 3.140625
- gain_back: float32 [4, 128], P('strip'), may hold values from 0.5 to 1
Outputs:
- first_pass: float32 [4, 64, 14336], P('strip', None, 'cross')
- solution: float32 [4, 64, 14336], P('strip', None, 'cross')
All inputs are finite; a program needn't handle non-finite values.
Results may differ from a plain program's by a relative error of at most 0.04.
Values may be sent and summed in bfloat16 or wider, within the bound.
A program may use at most 64 MiB of HBM per device.

v0:
```python
import jax
import jax.numpy as jnp
from jax import lax
from jax.sharding import PartitionSpec as P


def from_behind(shard, axis, by):
    peers = lax.axis_size(axis)
    pairs = [(i, i + by) for i in range(peers) if 0 <= i + by < peers]
    return lax.ppermute(shard, axis, pairs)


def rotate(values, cosine, sine, gain):
    real_part = values[:, 0, :]
    imag_part = values[:, 1, :]
    return jnp.stack(
        [
            gain * (cosine * real_part - sine * imag_part),
            gain * (sine * real_part + cosine * imag_part),
        ],
        axis=1,
    )


def factors(phase, gain):
    cosine = jnp.cos(phase)
    sine = jnp.sin(phase)
    return (cosine, sine, gain)


def section(source_rows, incoming, inverse, modes_in, modes_out):
    rows = source_rows.shape[0]
    half = incoming.shape[2]
    carried = incoming.reshape(rows, 2 * half)
    field = source_rows - jnp.dot(
        carried.astype(jnp.bfloat16), modes_in, preferred_element_type=jnp.float32
    )
    answer = jnp.dot(field.astype(jnp.bfloat16), inverse, preferred_element_type=jnp.float32)
    partial_modes = jnp.dot(
        answer.astype(jnp.bfloat16), modes_out, preferred_element_type=jnp.float32
    ).reshape(rows, 2, half)
    return (field, answer, partial_modes)


def sweep(source, inverse, modes_in, modes_out, phase, gain, step_by, count):
    angles, unknowns = source.shape
    rows = angles // count
    strips = lax.axis_size("strip")
    place = lax.axis_index("strip")
    if step_by == 1:
        order = place
    else:
        order = strips - 1 - place
    cosine, sine, gain = factors(phase, gain)
    start_state = jnp.zeros((rows, 2, cosine.shape[0]), jnp.float32)

    def tick(step, loop_state):
        state, solved, fields = loop_state
        batch = step - order
        valid = jnp.logical_and(batch >= 0, batch < count)
        field, answer, partial_modes = section(source, state, inverse, modes_in, modes_out)
        summed = lax.psum(partial_modes.astype(jnp.bfloat16), "cross").astype(jnp.float32)
        leaving = rotate(state, cosine, sine, gain) + summed
        arriving = from_behind(leaving.astype(jnp.bfloat16), "strip", step_by).astype(leaving.dtype)
        solved = jnp.where(valid, answer, solved)
        fields = jnp.where(valid, field, fields)
        return (arriving, solved, fields)

    empty = jnp.zeros((angles, unknowns), jnp.float32)
    final_state, solved, fields = lax.fori_loop(
        0, strips + count - 1, tick, (start_state, empty, empty)
    )
    return (solved, fields)


def body(
    rhs, inverse, dis_fwd, agg_fwd, phase_fwd, gain_fwd, dis_back, agg_back, phase_back, gain_back
):
    count = 1
    source = rhs[0].astype(jnp.float32)
    cluster_inverse = inverse[0, 0]
    first_pass, fields = sweep(
        source, cluster_inverse, dis_fwd[0, 0], agg_fwd[0], phase_fwd[0], gain_fwd[0], 1, count
    )
    solution, unused_fields = sweep(
        fields, cluster_inverse, dis_back[0, 0], agg_back[0], phase_back[0], gain_back[0], -1, count
    )
    return (first_pass[None], solution[None])


def solution(mesh):
    return jax.shard_map(
        body,
        mesh=mesh,
        in_specs=(
            P("strip", None, "cross"),
            P("strip", "cross", None, None),
            P("strip", "cross", None, None),
            P("strip", "cross", None),
            P("strip", None),
            P("strip", None),
            P("strip", "cross", None, None),
            P("strip", "cross", None),
            P("strip", None),
            P("strip", None),
        ),
        out_specs=(P("strip", None, "cross"), P("strip", None, "cross")),
        check_vma=False,
    )
```

profile of v0, /device:TPU:0, one launch (start us, length us, event | category | flops | bytes accessed | tf_op | source)
XLA Modules:
  0.0 278.0 jit_solution(4328669173243602671)
XLA Ops:
  1.3 1.7 bitcast_convert_fusion
  3.1 143.1 %while.34 = (s32[]{:T(128)}, f32[64,2,128]{2,0,1:T(8,128)S(1)}, f32[64,1792]{1,0:T(8,128)}, f32[64,1792]{1,0:T(8,128)S(1)}, f32[1,128]{1,0:T(1,128)}, /*index=5*...) while((s32[]{:T(128)}, f32[64,2,128]{2,0,1:T(8,128)S(1)}, ...), condition=%wide.region_2.3_spmd.clone, body=%wide.region_0.2_spmd.clone.sunk | while | flops 529498112 | bytes 15994644 | solution.py:70
  3.2 1.8 select_select_fusion.6
  4.9 4.9 %select_select_fusion.7 = (f32[64,1792]{1,0:T(8,128)}, bf16[64,1792]{1,0:T(8,128)(2,1)S(1)}) fusion(f32[64,1792]{1,0:T(8,128)} %get-tuple-element.718, pred[]{:T(512)S(6)} %compare.6, pred[]{:T(512)S(6)} %and.19, bf16[1792,1792]{1,0:T(8,128)(2,1)} %get-tuple-element.739, bf16[64,1792]{1,0:T(8,128)(2,1)S(1)} %get-tuple-element.681), kind=kOutput, calls=%fused_computation.4.clone.1 | convolution fusion | flops 411385856 | bytes 7798786 | tf_op jit(solution)/shard_map/while/body/eval_jaxpr/dot_general | solution.py:38
  10.1 25.6 %psum.26 = bf16[64,2,128]{2,0,1:T(8,128)(2,1)S(1)} all-reduce(bf16[64,2,128]{2,0,1:T(8,128)(2,1)S(1)} %bitcast.99), channel_id=1, replica_groups=mesh['strip'=4,'cross'=8] {'cross'}, use_global_device_ids=true, to_apply=%region_1.0 | all-reduce | flops 16384 | bytes 65536 | tf_op jit(solution)/shard_map/while/body/eval_jaxpr/psum | solution.py:62
  35.7 3.5 %collective-permute-start = (bf16[64,2,128]{2,0,1:T(8,128)(2,1)S(1)}, bf16[64,2,128]{2,0,1:T(8,128)(2,1)S(1)}, u32[]{:S(2)}, u32[]{:S(2)}) collective-permute-start(bf16[64,2,128]{2,0,1:T(8,128)(2,1)S(1)} %fusion.47), channel_id=1, source_target_pairs={{0,8},{8,16},{16,24},{1,9},{9,17},{17,25},{2,10},{10,18},{18,26},{... | collective-permute-start | bytes 98312 | tf_op jit(solution)/shard_map/while/body/eval_jaxpr/ppermute | solution.py:10
  40.8 1.7 select_select_fusion.6
  42.5 4.9 %select_select_fusion.7 = (f32[64,1792]{1,0:T(8,128)}, bf16[64,1792]{1,0:T(8,128)(2,1)S(1)}) fusion(f32[64,1792]{1,0:T(8,128)} %get-tuple-element.718, pred[]{:T(512)S(6)} %compare.6, pred[]{:T(512)S(6)} %and.19, bf16[1792,1792]{1,0:T(8,128)(2,1)} %get-tuple-element.739, bf16[64,1792]{1,0:T(8,128)(2,1)S(1)} %get-tuple-element.681), kind=kOutput, calls=%fused_computation.4.clone.1 | convolution fusion | flops 411385856 | bytes 7798786 | tf_op jit(solution)/shard_map/while/body/eval_jaxpr/dot_general | solution.py:38
  47.7 22.4 %psum.26 = bf16[64,2,128]{2,0,1:T(8,128)(2,1)S(1)} all-reduce(bf16[64,2,128]{2,0,1:T(8,128)(2,1)S(1)} %bitcast.99), channel_id=1, replica_groups=mesh['strip'=4,'cross'=8] {'cross'}, use_global_device_ids=true, to_apply=%region_1.0 | all-reduce | flops 16384 | bytes 65536 | tf_op jit(solution)/shard_map/while/body/eval_jaxpr/psum | solution.py:62
  70.1 4.2 %collective-permute-start = (bf16[64,2,128]{2,0,1:T(8,128)(2,1)S(1)}, bf16[64,2,128]{2,0,1:T(8,128)(2,1)S(1)}, u32[]{:S(2)}, u32[]{:S(2)}) collective-permute-start(bf16[64,2,128]{2,0,1:T(8,128)(2,1)S(1)} %fusion.47), channel_id=1, source_target_pairs={{0,8},{8,16},{16,24},{1,9},{9,17},{17,25},{2,10},{10,18},{18,26},{... | collective-permute-start | bytes 98312 | tf_op jit(solution)/shard_map/while/body/eval_jaxpr/ppermute | solution.py:10
  76.0 1.7 select_select_fusion.6
  77.6 4.9 %select_select_fusion.7 = (f32[64,1792]{1,0:T(8,128)}, bf16[64,1792]{1,0:T(8,128)(2,1)S(1)}) fusion(f32[64,1792]{1,0:T(8,128)} %get-tuple-element.718, pred[]{:T(512)S(6)} %compare.6, pred[]{:T(512)S(6)} %and.19, bf16[1792,1792]{1,0:T(8,128)(2,1)} %get-tuple-element.739, bf16[64,1792]{1,0:T(8,128)(2,1)S(1)} %get-tuple-element.681), kind=kOutput, calls=%fused_computation.4.clone.1 | convolution fusion | flops 411385856 | bytes 7798786 | tf_op jit(solution)/shard_map/while/body/eval_jaxpr/dot_general | solution.py:38
  82.8 22.4 %psum.26 = bf16[64,2,128]{2,0,1:T(8,128)(2,1)S(1)} all-reduce(bf16[64,2,128]{2,0,1:T(8,128)(2,1)S(1)} %bitcast.99), channel_id=1, replica_groups=mesh['strip'=4,'cross'=8] {'cross'}, use_global_device_ids=true, to_apply=%region_1.0 | all-reduce | flops 16384 | bytes 65536 | tf_op jit(solution)/shard_map/while/body/eval_jaxpr/psum | solution.py:62
  105.2 4.2 %collective-permute-start = (bf16[64,2,128]{2,0,1:T(8,128)(2,1)S(1)}, bf16[64,2,128]{2,0,1:T(8,128)(2,1)S(1)}, u32[]{:S(2)}, u32[]{:S(2)}) collective-permute-start(bf16[64,2,128]{2,0,1:T(8,128)(2,1)S(1)} %fusion.47), channel_id=1, source_target_pairs={{0,8},{8,16},{16,24},{1,9},{9,17},{17,25},{2,10},{10,18},{18,26},{... | collective-permute-start | bytes 98312 | tf_op jit(solution)/shard_map/while/body/eval_jaxpr/ppermute | solution.py:10
  109.5 1.6 collective-permute-done
  111.1 1.7 select_select_fusion.6
  112.8 4.9 %select_select_fusion.7 = (f32[64,1792]{1,0:T(8,128)}, bf16[64,1792]{1,0:T(8,128)(2,1)S(1)}) fusion(f32[64,1792]{1,0:T(8,128)} %get-tuple-element.718, pred[]{:T(512)S(6)} %compare.6, pred[]{:T(512)S(6)} %and.19, bf16[1792,1792]{1,0:T(8,128)(2,1)} %get-tuple-element.739, bf16[64,1792]{1,0:T(8,128)(2,1)S(1)} %get-tuple-element.681), kind=kOutput, calls=%fused_computation.4.clone.1 | convolution fusion | flops 411385856 | bytes 7798786 | tf_op jit(solution)/shard_map/while/body/eval_jaxpr/dot_general | solution.py:38
  118.0 22.4 %psum.26 = bf16[64,2,128]{2,0,1:T(8,128)(2,1)S(1)} all-reduce(bf16[64,2,128]{2,0,1:T(8,128)(2,1)S(1)} %bitcast.99), channel_id=1, replica_groups=mesh['strip'=4,'cross'=8] {'cross'}, use_global_device_ids=true, to_apply=%region_1.0 | all-reduce | flops 16384 | bytes 65536 | tf_op jit(solution)/shard_map/while/body/eval_jaxpr/psum | solution.py:62
  140.4 4.2 %collective-permute-start = (bf16[64,2,128]{2,0,1:T(8,128)(2,1)S(1)}, bf16[64,2,128]{2,0,1:T(8,128)(2,1)S(1)}, u32[]{:S(2)}, u32[]{:S(2)}) collective-permute-start(bf16[64,2,128]{2,0,1:T(8,128)(2,1)S(1)} %fusion.47), channel_id=1, source_target_pairs={{0,8},{8,16},{16,24},{1,9},{9,17},{17,25},{2,10},{10,18},{18,26},{... | collective-permute-start | bytes 98312 | tf_op jit(solution)/shard_map/while/body/eval_jaxpr/ppermute | solution.py:10
  146.3 131.0 %while.35 = (s32[]{:T(128)}, f32[64,2,128]{2,0,1:T(8,128)S(1)}, f32[64,1792]{1,0:T(8,128)S(1)}, f32[1,128]{1,0:T(1,128)S(1)}, f32[128]{0:T(128)S(1)}, /*index=5*...) while((s32[]{:T(128)}, f32[64,2,128]{2,0,1:T(8,128)S(1)}, ...), condition=%wide.region_5.6_spmd.clone, body=%wide.region_3.5_spmd.clone.sunk | while | flops 529268736 | bytes 10946258 | solution.py:70
  146.4 4.1 %select_select_fusion.8 = (f32[64,1792]{1,0:T(8,128)S(1)}, bf16[64,1792]{1,0:T(8,128)(2,1)S(1)}) fusion(f32[64,1792]{1,0:T(8,128)S(1)} %get-tuple-element.759, pred[]{:T(512)S(6)} %compare.7, pred[]{:T(512)S(6)} %and.20, bf16[1792,1792]{1,0:T(8,128)(2,1)} %get-tuple-element.778, f32[64,1792]{1,0:T(8,128)S(1)} %get-tuple-element.777, ...), kind=kOutput, calls=%fused_computation.22.clone.1 | convolution fusion | flops 470335488 | bytes 8978434 | tf_op jit(solution)/shard_map/while/body/eval_jaxpr/dot_general | solution.py:38
  150.8 22.4 %psum.27 = bf16[64,2,128]{2,0,1:T(8,128)(2,1)S(1)} all-reduce(bf16[64,2,128]{2,0,1:T(8,128)(2,1)S(1)} %bitcast.100), channel_id=1, replica_groups=mesh['strip'=4,'cross'=8] {'cross'}, use_global_device_ids=true, to_apply=%region_4.4 | all-reduce | flops 16384 | bytes 65536 | tf_op jit(solution)/shard_map/while/body/eval_jaxpr/psum | solution.py:62
  174.5 4.8 %collective-permute-done.1 = bf16[64,2,128]{2,0,1:T(8,128)(2,1)S(1)} collective-permute-done((bf16[64,2,128]{2,0,1:T(8,128)(2,1)S(1)}, bf16[64,2,128]{2,0,1:T(8,128)(2,1)S(1)}, u32[]{:S(2)}, u32[]{:S(2)}) %collective-permute-start.1) | collective-permute-done | bytes 32800 | tf_op jit(solution)/shard_map/while/body/eval_jaxpr/ppermute | solution.py:10
  179.3 4.1 %select_select_fusion.8 = (f32[64,1792]{1,0:T(8,128)S(1)}, bf16[64,1792]{1,0:T(8,128)(2,1)S(1)}) fusion(f32[64,1792]{1,0:T(8,128)S(1)} %get-tuple-element.759, pred[]{:T(512)S(6)} %compare.7, pred[]{:T(512)S(6)} %and.20, bf16[1792,1792]{1,0:T(8,128)(2,1)} %get-tuple-element.778, f32[64,1792]{1,0:T(8,128)S(1)} %get-tuple-element.777, ...), kind=kOutput, calls=%fused_computation.22.clone.1 | convolution fusion | flops 470335488 | bytes 8978434 | tf_op jit(solution)/shard_map/while/body/eval_jaxpr/dot_general | solution.py:38
  183.7 22.4 %psum.27 = bf16[64,2,128]{2,0,1:T(8,128)(2,1)S(1)} all-reduce(bf16[64,2,128]{2,0,1:T(8,128)(2,1)S(1)} %bitcast.100), channel_id=1, replica_groups=mesh['strip'=4,'cross'=8] {'cross'}, use_global_device_ids=true, to_apply=%region_4.4 | all-reduce | flops 16384 | bytes 65536 | tf_op jit(solution)/shard_map/while/body/eval_jaxpr/psum | solution.py:62
  207.4 4.5 %collective-permute-done.1 = bf16[64,2,128]{2,0,1:T(8,128)(2,1)S(1)} collective-permute-done((bf16[64,2,128]{2,0,1:T(8,128)(2,1)S(1)}, bf16[64,2,128]{2,0,1:T(8,128)(2,1)S(1)}, u32[]{:S(2)}, u32[]{:S(2)}) %collective-permute-start.1) | collective-permute-done | bytes 32800 | tf_op jit(solution)/shard_map/while/body/eval_jaxpr/ppermute | solution.py:10
  212.0 4.1 %select_select_fusion.8 = (f32[64,1792]{1,0:T(8,128)S(1)}, bf16[64,1792]{1,0:T(8,128)(2,1)S(1)}) fusion(f32[64,1792]{1,0:T(8,128)S(1)} %get-tuple-element.759, pred[]{:T(512)S(6)} %compare.7, pred[]{:T(512)S(6)} %and.20, bf16[1792,1792]{1,0:T(8,128)(2,1)} %get-tuple-element.778, f32[64,1792]{1,0:T(8,128)S(1)} %get-tuple-element.777, ...), kind=kOutput, calls=%fused_computation.22.clone.1 | convolution fusion | flops 470335488 | bytes 8978434 | tf_op jit(solution)/shard_map/while/body/eval_jaxpr/dot_general | solution.py:38
  216.4 22.4 %psum.27 = bf16[64,2,128]{2,0,1:T(8,128)(2,1)S(1)} all-reduce(bf16[64,2,128]{2,0,1:T(8,128)(2,1)S(1)} %bitcast.100), channel_id=1, replica_groups=mesh['strip'=4,'cross'=8] {'cross'}, use_global_device_ids=true, to_apply=%region_4.4 | all-reduce | flops 16384 | bytes 65536 | tf_op jit(solution)/shard_map/while/body/eval_jaxpr/psum | solution.py:62
  240.1 4.5 %collective-permute-done.1 = bf16[64,2,128]{2,0,1:T(8,128)(2,1)S(1)} collective-permute-done((bf16[64,2,128]{2,0,1:T(8,128)(2,1)S(1)}, bf16[64,2,128]{2,0,1:T(8,128)(2,1)S(1)}, u32[]{:S(2)}, u32[]{:S(2)}) %collective-permute-start.1) | collective-permute-done | bytes 32800 | tf_op jit(solution)/shard_map/while/body/eval_jaxpr/ppermute | solution.py:10
  244.6 4.1 %select_select_fusion.8 = (f32[64,1792]{1,0:T(8,128)S(1)}, bf16[64,1792]{1,0:T(8,128)(2,1)S(1)}) fusion(f32[64,1792]{1,0:T(8,128)S(1)} %get-tuple-element.759, pred[]{:T(512)S(6)} %compare.7, pred[]{:T(512)S(6)} %and.20, bf16[1792,1792]{1,0:T(8,128)(2,1)} %get-tuple-element.778, f32[64,1792]{1,0:T(8,128)S(1)} %get-tuple-element.777, ...), kind=kOutput, calls=%fused_computation.22.clone.1 | convolution fusion | flops 470335488 | bytes 8978434 | tf_op jit(solution)/shard_map/while/body/eval_jaxpr/dot_general | solution.py:38
  249.1 22.4 %psum.27 = bf16[64,2,128]{2,0,1:T(8,128)(2,1)S(1)} all-reduce(bf16[64,2,128]{2,0,1:T(8,128)(2,1)S(1)} %bitcast.100), channel_id=1, replica_groups=mesh['strip'=4,'cross'=8] {'cross'}, use_global_device_ids=true, to_apply=%region_4.4 | all-reduce | flops 16384 | bytes 65536 | tf_op jit(solution)/shard_map/while/body/eval_jaxpr/psum | solution.py:62
  272.8 4.5 %collective-permute-done.1 = bf16[64,2,128]{2,0,1:T(8,128)(2,1)S(1)} collective-permute-done((bf16[64,2,128]{2,0,1:T(8,128)(2,1)S(1)}, bf16[64,2,128]{2,0,1:T(8,128)(2,1)S(1)}, u32[]{:S(2)}, u32[]{:S(2)}) %collective-permute-start.1) | collective-permute-done | bytes 32800 | tf_op jit(solution)/shard_map/while/body/eval_jaxpr/ppermute | solution.py:10
  (88 shorter events, 14.0 us)
Async XLA Ops:
  3.1 143.2 %copy-start.6 = (f32[1,128]{1,0:T(1,128)S(1)}, f32[1,128]{1,0:T(1,128)}, u32[]{:S(2)}) copy-start(f32[1,128]{1,0:T(1,128)} %param.22) | copy-start | bytes 1540
  3.1 143.2 %copy-start = (bf16[1,1,256,1792]{3,2,1,0:T(8,128)(2,1)S(1)}, bf16[1,1,256,1792]{3,2,1,0:T(8,128)(2,1)}, u32[]{:S(2)}) copy-start(bf16[1,1,256,1792]{3,2,1,0:T(8,128)(2,1)} %param.20) | copy-start | bytes 2752516
  3.1 143.2 %copy-start.2 = (bf16[1,1792,256]{2,1,0:T(8,128)(2,1)S(1)}, bf16[1,1792,256]{2,1,0:T(8,128)(2,1)}, u32[]{:S(2)}) copy-start(bf16[1,1792,256]{2,1,0:T(8,128)(2,1)} %param.21) | copy-start | bytes 2752516
  3.1 143.2 %copy-start.5 = (f32[1,128]{1,0:T(1,128)S(1)}, f32[1,128]{1,0:T(1,128)}, u32[]{:S(2)}) copy-start(f32[1,128]{1,0:T(1,128)} %param.23) | copy-start | bytes 1540
  3.1 6.7 %copy-start.1 = (bf16[1792,256]{1,0:T(8,128)(2,1)S(1)}, bf16[1792,256]{1,0:T(8,128)(2,1)}, u32[]{:S(2)}) copy-start(bf16[1792,256]{1,0:T(8,128)(2,1)} %get-tuple-element.740) | copy-start | bytes 2752516 | tf_op jit(solution)/shard_map/while
  3.1 32.5 %copy-start.4 = (f32[1,128]{1,0:T(1,128)S(1)}, f32[1,128]{1,0:T(1,128)}, u32[]{:S(2)}) copy-start(f32[1,128]{1,0:T(1,128)} %get-tuple-element.734) | copy-start | bytes 1540 | tf_op jit(solution)/shard_map/while
  35.7 5.1 %collective-permute-start = (bf16[64,2,128]{2,0,1:T(8,128)(2,1)S(1)}, bf16[64,2,128]{2,0,1:T(8,128)(2,1)S(1)}, u32[]{:S(2)}, u32[]{:S(2)}) collective-permute-start(bf16[64,2,128]{2,0,1:T(8,128)(2,1)S(1)} %fusion.47), channel_id=1, source_target_pairs={{0,8},{8,16},{16,24},{1,9},{9,17},{17,25},{2,10},{10,18},{18,26},{... | collective-permute-start | bytes 98312 | tf_op jit(solution)/shard_map/while/body/eval_jaxpr/ppermute | solution.py:10
  40.8 6.6 %copy-start.1 = (bf16[1792,256]{1,0:T(8,128)(2,1)S(1)}, bf16[1792,256]{1,0:T(8,128)(2,1)}, u32[]{:S(2)}) copy-start(bf16[1792,256]{1,0:T(8,128)(2,1)} %get-tuple-element.740) | copy-start | bytes 2752516 | tf_op jit(solution)/shard_map/while
  40.8 29.3 %copy-start.4 = (f32[1,128]{1,0:T(1,128)S(1)}, f32[1,128]{1,0:T(1,128)}, u32[]{:S(2)}) copy-start(f32[1,128]{1,0:T(1,128)} %get-tuple-element.734) | copy-start | bytes 1540 | tf_op jit(solution)/shard_map/while
  70.1 5.8 %collective-permute-start = (bf16[64,2,128]{2,0,1:T(8,128)(2,1)S(1)}, bf16[64,2,128]{2,0,1:T(8,128)(2,1)S(1)}, u32[]{:S(2)}, u32[]{:S(2)}) collective-permute-start(bf16[64,2,128]{2,0,1:T(8,128)(2,1)S(1)} %fusion.47), channel_id=1, source_target_pairs={{0,8},{8,16},{16,24},{1,9},{9,17},{17,25},{2,10},{10,18},{18,26},{... | collective-permute-start | bytes 98312 | tf_op jit(solution)/shard_map/while/body/eval_jaxpr/ppermute | solution.py:10
  75.9 6.6 %copy-start.1 = (bf16[1792,256]{1,0:T(8,128)(2,1)S(1)}, bf16[1792,256]{1,0:T(8,128)(2,1)}, u32[]{:S(2)}) copy-start(bf16[1792,256]{1,0:T(8,128)(2,1)} %get-tuple-element.740) | copy-start | bytes 2752516 | tf_op jit(solution)/shard_map/while
  75.9 29.3 %copy-start.4 = (f32[1,128]{1,0:T(1,128)S(1)}, f32[1,128]{1,0:T(1,128)}, u32[]{:S(2)}) copy-start(f32[1,128]{1,0:T(1,128)} %get-tuple-element.734) | copy-start | bytes 1540 | tf_op jit(solution)/shard_map/while
  105.2 5.8 %collective-permute-start = (bf16[64,2,128]{2,0,1:T(8,128)(2,1)S(1)}, bf16[64,2,128]{2,0,1:T(8,128)(2,1)S(1)}, u32[]{:S(2)}, u32[]{:S(2)}) collective-permute-start(bf16[64,2,128]{2,0,1:T(8,128)(2,1)S(1)} %fusion.47), channel_id=1, source_target_pairs={{0,8},{8,16},{16,24},{1,9},{9,17},{17,25},{2,10},{10,18},{18,26},{... | collective-permute-start | bytes 98312 | tf_op jit(solution)/shard_map/while/body/eval_jaxpr/ppermute | solution.py:10
  111.1 6.6 %copy-start.1 = (bf16[1792,256]{1,0:T(8,128)(2,1)S(1)}, bf16[1792,256]{1,0:T(8,128)(2,1)}, u32[]{:S(2)}) copy-start(bf16[1792,256]{1,0:T(8,128)(2,1)} %get-tuple-element.740) | copy-start | bytes 2752516 | tf_op jit(solution)/shard_map/while
  111.1 29.3 %copy-start.4 = (f32[1,128]{1,0:T(1,128)S(1)}, f32[1,128]{1,0:T(1,128)}, u32[]{:S(2)}) copy-start(f32[1,128]{1,0:T(1,128)} %get-tuple-element.734) | copy-start | bytes 1540 | tf_op jit(solution)/shard_map/while
  140.4 5.8 %collective-permute-start = (bf16[64,2,128]{2,0,1:T(8,128)(2,1)S(1)}, bf16[64,2,128]{2,0,1:T(8,128)(2,1)S(1)}, u32[]{:S(2)}, u32[]{:S(2)}) collective-permute-start(bf16[64,2,128]{2,0,1:T(8,128)(2,1)S(1)} %fusion.47), channel_id=1, source_target_pairs={{0,8},{8,16},{16,24},{1,9},{9,17},{17,25},{2,10},{10,18},{18,26},{... | collective-permute-start | bytes 98312 | tf_op jit(solution)/shard_map/while/body/eval_jaxpr/ppermute | solution.py:10
  173.2 6.1 %collective-permute-start.1 = (bf16[64,2,128]{2,0,1:T(8,128)(2,1)S(1)}, bf16[64,2,128]{2,0,1:T(8,128)(2,1)S(1)}, u32[]{:S(2)}, u32[]{:S(2)}) collective-permute-start(bf16[64,2,128]{2,0,1:T(8,128)(2,1)S(1)} %fusion.54), channel_id=1, source_target_pairs={{8,0},{16,8},{24,16},{9,1},{17,9},{25,17},{10,2},{18,10},{26,18},{... | collective-permute-start | bytes 98312 | tf_op jit(solution)/shard_map/while/body/eval_jaxpr/ppermute | solution.py:10
  206.1 5.8 %collective-permute-start.1 = (bf16[64,2,128]{2,0,1:T(8,128)(2,1)S(1)}, bf16[64,2,128]{2,0,1:T(8,128)(2,1)S(1)}, u32[]{:S(2)}, u32[]{:S(2)}) collective-permute-start(bf16[64,2,128]{2,0,1:T(8,128)(2,1)S(1)} %fusion.54), channel_id=1, source_target_pairs={{8,0},{16,8},{24,16},{9,1},{17,9},{25,17},{10,2},{18,10},{26,18},{... | collective-permute-start | bytes 98312 | tf_op jit(solution)/shard_map/while/body/eval_jaxpr/ppermute | solution.py:10
  238.8 5.8 %collective-permute-start.1 = (bf16[64,2,128]{2,0,1:T(8,128)(2,1)S(1)}, bf16[64,2,128]{2,0,1:T(8,128)(2,1)S(1)}, u32[]{:S(2)}, u32[]{:S(2)}) collective-permute-start(bf16[64,2,128]{2,0,1:T(8,128)(2,1)S(1)} %fusion.54), channel_id=1, source_target_pairs={{8,0},{16,8},{24,16},{9,1},{17,9},{25,17},{10,2},{18,10},{26,18},{... | collective-permute-start | bytes 98312 | tf_op jit(solution)/shard_map/while/body/eval_jaxpr/ppermute | solution.py:10
  271.5 5.8 %collective-permute-start.1 = (bf16[64,2,128]{2,0,1:T(8,128)(2,1)S(1)}, bf16[64,2,128]{2,0,1:T(8,128)(2,1)S(1)}, u32[]{:S(2)}, u32[]{:S(2)}) collective-permute-start(bf16[64,2,128]{2,0,1:T(8,128)(2,1)S(1)} %fusion.54), channel_id=1, source_target_pairs={{8,0},{16,8},{24,16},{9,1},{17,9},{25,17},{10,2},{18,10},{26,18},{... | collective-permute-start | bytes 98312 | tf_op jit(solution)/shard_map/while/body/eval_jaxpr/ppermute | solution.py:10
  277.3 0.8 copy-start.3
where the time goes:
time: 279 us; the launch traced here: 278 us
  blocking collectives  182 us (65%)
  matrix products  45 us (16%)
  waiting for transfers between devices  24.7 us (9%)
  starting transfers between devices  21.3 us (8%)
    psum x8, blocking collectives, tick(): lax.psum(partial_modes.astype(jnp.bfloat16), 'cross').astype(jnp.float32)  182 us
    dot_general x8, matrix products, section(): jnp.dot(field.astype(jnp.bfloat16), inverse, preferred_element_type=jnp.f...  36 us
    ppermute x8, waiting for transfers between devices, from_behind(): return lax.ppermute(shard, axis, pairs)  24.7 us
    ppermute x8, starting transfers between devices, from_behind(): return lax.ppermute(shard, axis, pairs)  21.3 us
    dot_general x4, matrix products, section(): jnp.dot(carried.astype(jnp.bfloat16), modes_in, preferred_element_type=jn...  6.77 us
  transfers between devices with their start and end apart: 8, of which 8 were waited for; matrix products, arithmetic and copies ran while one was open for 0% of the time, Pallas kernels for 0%

commit v1 on v0

v1 whole, which is shorter than its diff:
```python
import functools

import jax
import jax.numpy as jnp
from jax import lax
from jax.experimental import pallas as pl
from jax.experimental.pallas import tpu as pltpu
from jax.sharding import PartitionSpec as P

MESH = pl.DeviceIdType.MESH
BF = jnp.bfloat16
F32 = jnp.float32
T_RS, B_RS, T_AG, N_RS, N_AG, E_RS, C_ON, D_ON = range(8)


def dot(a, b):
    return jnp.dot(a, b, preferred_element_type=F32)


def kernel(
    strips, n, width,
    rhs, inverse, dis_fwd, agg_fwd, phase_fwd, gain_fwd, dis_back, agg_back, phase_back, gain_back,
    first_ref, second_ref,
    x_f, x_b, inv, agg_f, agg_b, p, u_f, u_b,
    t_own, t_out, t_in, n_own, n_out, n_in, t_all, n_all,
    b_own, b_out, b_in, e_own, e_out, e_in, b_red, e_red,
    c_out, c_all, d_out, d_all,
    load_sem, sems,
):
    s = lax.axis_index("strip")
    me = lax.axis_index("cross")
    is_first = s == 0
    is_last = s == strips - 1
    inner = jnp.logical_and(s > 0, s < strips - 1)
    angles = rhs.shape[1]
    modes = agg_f.shape[1]
    half = modes // 2
    unk = p.shape[1]
    blocks = unk // width
    rows = angles // n

    loads = [
        pltpu.make_async_copy(rhs.at[0], x_f.at[pl.ds(0, angles)], load_sem.at[0]),
        pltpu.make_async_copy(dis_fwd.at[0, 0], x_f.at[pl.ds(angles, modes)], load_sem.at[1]),
        pltpu.make_async_copy(agg_fwd.at[0], agg_f, load_sem.at[2]),
        pltpu.make_async_copy(dis_back.at[0, 0], x_b, load_sem.at[3]),
        pltpu.make_async_copy(agg_back.at[0], agg_b, load_sem.at[4]),
    ]
    inv_loads = [
        pltpu.make_async_copy(
            inverse.at[0, 0, :, pl.ds(j * width, width)], inv.at[j], load_sem.at[5 + j]
        )
        for j in range(blocks)
    ]
    loads[0].start()
    loads[1].start()
    for copy in inv_loads:
        copy.start()
    for copy in loads[2:]:
        copy.start()

    barrier = pltpu.get_barrier_semaphore()

    def greet(strip, peer):
        pl.semaphore_signal(barrier, inc=1, device_id=(strip, peer), device_id_type=MESH)

    def others(fn):
        def step(j, carry):
            fn(lax.rem(me + j, n))
            return carry
        lax.fori_loop(1, n, step, 0)

    def everyone(fn):
        def step(j, carry):
            fn(lax.rem(me + j, n))
            return carry
        lax.fori_loop(0, n, step, 0)

    others(lambda peer: greet(s, peer))

    @pl.when(s > 0)
    def _():
        everyone(lambda peer: greet(s - 1, peer))

    @pl.when(s < strips - 1)
    def _():
        everyone(lambda peer: greet(s + 1, peer))

    def remote(kind, src, dst, strip, peer):
        return pltpu.make_async_remote_copy(
            src_ref=src,
            dst_ref=dst,
            send_sem=sems.at[kind, 0, peer],
            recv_sem=sems.at[kind, 1, me],
            device_id=(strip, peer),
            device_id_type=MESH,
        )

    def arrived(kind, dst, peer):
        pltpu.make_async_remote_copy(
            src_ref=dst.at[peer],
            dst_ref=dst.at[peer],
            send_sem=sems.at[kind, 0, peer],
            recv_sem=sems.at[kind, 1, peer],
            device_id=(s, peer),
            device_id_type=MESH,
        ).wait_recv()

    def scatter(kind, out, into):
        others(lambda peer: remote(kind, out.at[peer], into.at[me], s, peer).start())

    def scatter_sent(kind, out, into):
        others(lambda peer: remote(kind, out.at[peer], into.at[me], s, peer).wait_send())

    def total(kind, own, into):
        others(lambda peer: arrived(kind, into, peer))
        value = own[me]
        for j in range(1, n):
            value = value + into[lax.rem(me + j, n)].astype(F32)
        return value

    def share(kind, buf):
        others(lambda peer: remote(kind, buf.at[me], buf.at[me], s, peer).start())

    def share_sent(kind, buf):
        others(lambda peer: remote(kind, buf.at[me], buf.at[me], s, peer).wait_send())

    def pass_on(kind, src, buf, strip):
        everyone(lambda peer: remote(kind, src, buf.at[me], strip, peer).start())

    def passed_on(kind, src, buf, strip):
        everyone(lambda peer: remote(kind, src, buf.at[me], strip, peer).wait_send())

    def split(value, own, out):
        part = value.shape[0] // n
        for k in range(n):
            piece = value[k * part:(k + 1) * part]
            own[k] = piece
            out[k] = piece.astype(BF)

    def joined(buf):
        return jnp.concatenate([buf[k] for k in range(n)], axis=0)

    def rotated(value, phase, gain):
        real, imag = value[:, :half], value[:, half:]
        cosine, sine, g = jnp.cos(phase[...]), jnp.sin(phase[...]), gain[...]
        return jnp.concatenate(
            [g * (cosine * real - sine * imag), g * (sine * real + cosine * imag)], axis=1
        )

    loads[0].wait()
    loads[1].wait()
    for j in range(blocks):
        inv_loads[j].wait()
        product = dot(x_f[...], inv[j])
        p[:, j * width:(j + 1) * width] = product[:angles]
        u_f[:, j * width:(j + 1) * width] = product[angles:].astype(BF)
    loads[2].wait()

    @pl.when(inner)
    def _():
        split(dot(u_f[...], agg_f[...]), t_own, t_out)

    @pl.when(s < strips - 1)
    def _():
        split(dot(p[...].astype(BF), agg_f[...]), b_own, b_out)

    greeted = (n - 1) + jnp.where(s > 0, n, 0) + jnp.where(s < strips - 1, n, 0)
    pl.semaphore_wait(barrier, greeted)

    @pl.when(s < strips - 1)
    def _():
        scatter(B_RS, b_out, b_in)

    @pl.when(inner)
    def _():
        scatter(T_RS, t_out, t_in)

    loads[3].wait()
    loads[4].wait()

    @pl.when(is_last)
    def _():
        split(dot(p[...].astype(BF), agg_b[...]), e_own, e_out)
        scatter(E_RS, e_out, e_in)
        split(dot(u_f[...], agg_b[...]), n_own, n_out)

    @pl.when(s < strips - 1)
    def _():
        for j in range(blocks):
            u_b[:, j * width:(j + 1) * width] = dot(x_b[...], inv[j]).astype(BF)

    @pl.when(inner)
    def _():
        split(dot(u_b[...], agg_b[...]), n_own, n_out)

    @pl.when(s < strips - 1)
    def _():
        b_red[...] = total(B_RS, b_own, b_in)

    @pl.when(is_first)
    def _():
        c_out[...] = b_red[...].astype(BF)
        pass_on(C_ON, c_out, c_all, s + 1)

    @pl.when(inner)
    def _():
        t_all[me] = total(T_RS, t_own, t_in).astype(BF)
        share(T_AG, t_all)

    @pl.when(s > 0)
    def _():
        scatter(N_RS, n_out, n_in)

    @pl.when(inner)
    def _():
        others(lambda peer: arrived(T_AG, t_all, peer))
        arrived(C_ON, c_all, me)
        held = c_all[me]
        leaving = rotated(held.astype(F32), phase_fwd, gain_fwd) + b_red[...]
        leaving = leaving - dot(held, joined(t_all))
        c_out[...] = leaving.astype(BF)
        pass_on(C_ON, c_out, c_all, s + 1)

    @pl.when(s > 0)
    def _():
        n_all[me] = total(N_RS, n_own, n_in).astype(BF)
        share(N_AG, n_all)

    @pl.when(is_last)
    def _():
        e_red[...] = total(E_RS, e_own, e_in)
        others(lambda peer: arrived(N_AG, n_all, peer))
        arrived(C_ON, c_all, me)
        d_out[...] = (e_red[...] - dot(c_all[me], joined(n_all))).astype(BF)
        pass_on(D_ON, d_out, d_all, s - 1)

    @pl.when(is_first)
    def _():
        first_ref[0] = p[...]

    @pl.when(s > 0)
    def _():
        others(lambda peer: arrived(C_ON, c_all, peer))
        first_ref[0] = p[...] - dot(joined(c_all), u_f[...])

    @pl.when(inner)
    def _():
        split(dot(first_ref[0].astype(BF), agg_b[...]), e_own, e_out)
        scatter(E_RS, e_out, e_in)
        others(lambda peer: arrived(N_AG, n_all, peer))
        e_red[...] = total(E_RS, e_own, e_in)
        arrived(D_ON, d_all, me)
        held = d_all[me]
        leaving = rotated(held.astype(F32), phase_back, gain_back) + e_red[...]
        leaving = leaving - dot(held, joined(n_all))
        d_out[...] = leaving.astype(BF)
        pass_on(D_ON, d_out, d_all, s - 1)

    @pl.when(is_last)
    def _():
        second_ref[0] = first_ref[0]

    @pl.when(is_first)
    def _():
        arrived(D_ON, d_all, me)

    @pl.when(s < strips - 1)
    def _():
        others(lambda peer: arrived(D_ON, d_all, peer))
        second_ref[0] = first_ref[0] - dot(joined(d_all), u_b[...])

    @pl.when(inner)
    def _():
        scatter_sent(T_RS, t_out, t_in)
        share_sent(T_AG, t_all)

    @pl.when(s < strips - 1)
    def _():
        scatter_sent(B_RS, b_out, b_in)
        passed_on(C_ON, c_out, c_all, s + 1)

    @pl.when(s > 0)
    def _():
        scatter_sent(N_RS, n_out, n_in)
        share_sent(N_AG, n_all)
        scatter_sent(E_RS, e_out, e_in)
        passed_on(D_ON, d_out, d_all, s - 1)


def body(strips, n, rhs, inverse, dis_fwd, agg_fwd, phase_fwd, gain_fwd, dis_back, agg_back, phase_back, gain_back):
    _, angles, unk = rhs.shape
    modes = agg_fwd.shape[2]
    width = 256 if unk % 256 == 0 else unk
    blocks = unk // width
    rows, part = angles // n, modes // n
    hbm = pl.BlockSpec(memory_space=pl.ANY)
    vmem = pl.BlockSpec(memory_space=pltpu.VMEM)
    out = jax.ShapeDtypeStruct((1, angles, unk), F32)
    return pl.pallas_call(
        functools.partial(kernel, strips, n, width),
        out_shape=(out, out),
        in_specs=[hbm, hbm, hbm, hbm, vmem, vmem, hbm, hbm, vmem, vmem],
        out_specs=(vmem, vmem),
        scratch_shapes=[
            pltpu.VMEM((angles + modes, unk), BF),
            pltpu.VMEM((modes, unk), BF),
            pltpu.VMEM((blocks, unk, width), BF),
            pltpu.VMEM((unk, modes), BF),
            pltpu.VMEM((unk, modes), BF),
            pltpu.VMEM((angles, unk), F32),
            pltpu.VMEM((modes, unk), BF),
            pltpu.VMEM((modes, unk), BF),
        ]
        + [pltpu.VMEM((n, part, modes), kind) for kind in (F32, BF, BF) * 2 + (BF, BF)]
        + [pltpu.VMEM((n, rows, modes), kind) for kind in (F32, BF, BF) * 2]
        + [pltpu.VMEM((rows, modes), F32)] * 2
        + [pltpu.VMEM((rows, modes), BF), pltpu.VMEM((n, rows, modes), BF)] * 2
        + [pltpu.SemaphoreType.DMA((5 + blocks,)), pltpu.SemaphoreType.DMA((8, 2, n))],
        compiler_params=pltpu.CompilerParams(
            collective_id=0, has_side_effects=True, vmem_limit_bytes=60 * 1024 * 1024
        ),
    )(rhs, inverse, dis_fwd, agg_fwd, phase_fwd, gain_fwd, dis_back, agg_back, phase_back, gain_back)


def solution(mesh):
    strips, n = mesh.shape["strip"], mesh.shape["cross"]
    return jax.shard_map(
        functools.partial(body, strips, n),
        mesh=mesh,
        in_specs=(
            P("strip", None, "cross"),
            P("strip", "cross", None, None),
            P("strip", "cross", None, None),
            P("strip", "cross", None),
            P("strip", None),
            P("strip", None),
            P("strip", "cross", None, None),
            P("strip", "cross", None),
            P("strip", None),
            P("strip", None),
        ),
        out_specs=(P("strip", None, "cross"), P("strip", None, "cross")),
        check_vma=False,
    )
```

time: 279 us -> 40.2 us (0.14)
  blocking collectives: 182 us -> 0 us
  matrix products: 45 us -> 0 us
  Pallas kernels: 0 us -> 35.8 us
  waiting for transfers between devices: 24.7 us -> 0 us
  starting transfers between devices: 21.3 us -> 0 us
    psum x8 -> x0, blocking collectives: 182 us -> none  [tick(): lax.psum(partial_modes.astype(jnp.bfloat16), 'cross').astype(jnp.float32)]
    dot_general x20 -> x0, matrix products: 45 us -> none  [the longest x8 36 us: section(): jnp.dot(field.astype(jnp.bfloat16), inverse, preferred_element_type=jnp.f...]
    pallas_call x0 -> x1, Pallas kernels: none -> 35.8 us  [body(): pl.pallas_call(functools.partial(kernel, strips, n, width), out_shape=(ou...]
    ppermute x8 -> x0, waiting for transfers between devices: 24.7 us -> none  [from_behind(): return lax.ppermute(shard, axis, pairs)]
    ppermute x8 -> x0, starting transfers between devices: 21.3 us -> none  [from_behind(): return lax.ppermute(shard, axis, pairs)]
    unnamed x10 -> x2, local copies, waits for them, and re-layouts: 0.78 us -> 3.63 us
  transfers between devices with their start and end apart: 8 -> 0, of which waited for: 8 -> 0; matrix products, arithmetic and copies ran while one was open for 0% -> 0% of each run, Pallas kernels for 0% -> 0%
where the time goes in v1:
time: 40.2 us; the launch traced here: 40 us
  Pallas kernels  35.8 us (89%)
  local copies, waits for them, and re-layouts  3.63 us (9%)
  between operations  0.64 us (2%)
    pallas_call x1, Pallas kernels, body(): pl.pallas_call(functools.partial(kernel, strips, n, width), out_shape=(ou...  35.8 us
    unnamed x2, local copies, waits for them, and re-layouts  3.63 us

profile of v1, /device:TPU:0, one launch (start us, length us, event | category | flops | bytes accessed | tf_op | source)
XLA Modules:
  0.0 40.0 jit_solution(13051513300803728263)
XLA Ops:
  0.6 35.8 %shard_map.113 = (f32[1,64,1792]{2,1,0:T(8,128)}, f32[1,64,1792]{2,1,0:T(8,128)}) custom-call(bf16[1,64,1792]{2,1,0:T(8,128)(2,1)} %rhs.1, bf16[1,1,1792,1792]{3,2,1,0:T(8,128)(2,1)} %inverse.1, bf16[1,1,256,1792]{3,2,1,0:T(8,128)(2,1)} %dis_fwd.1, bf16[1,1792,256]{2,1,0:T(8,128)(2,1)} %agg_fwd.1, f32[1,128]{1,0:T(1,128)} %phase_fwd.1, f32[1,128]{1,0:T(1,128)} %gain_fwd.1, ...), custom_call_target="tpu_custom_call" | custom-call | tf_op jit(solution)/shard_map/pallas_call | solution.py:300
  36.4 1.8 %copy.14 = f32[1,64,1792]{2,1,0:T(8,128)} copy(f32[1,64,1792]{2,1,0:T(8,128)} %get-tuple-element.4) | data formatting | bytes 917504
  38.2 1.8 %copy.15 = f32[1,64,1792]{2,1,0:T(8,128)} copy(f32[1,64,1792]{2,1,0:T(8,128)} %get-tuple-element.5) | data formatting | bytes 917504

commit v2 on v1

--- a/solution.py
+++ b/solution.py
@@ -10,7 +10,8 @@
 MESH = pl.DeviceIdType.MESH
 BF = jnp.bfloat16
 F32 = jnp.float32
-T_RS, B_RS, T_AG, N_RS, N_AG, E_RS, C_ON, D_ON = range(8)
+KINDS = 11
+T_RS, B_RS, T_AG, N_RS, N_AG, E_RS, C_IN, C_ON, C_SH, D_ON, D_SH = range(KINDS)
 
 
 def dot(a, b):
@@ -23,9 +24,9 @@
     first_ref, second_ref,
     x_f, x_b, inv, agg_f, agg_b, p, u_f, u_b,
     t_own, t_out, t_in, n_own, n_out, n_in, t_all, n_all,
-    b_own, b_out, b_in, e_own, e_out, e_in, b_red, e_red,
+    b_own, b_out, b_in, e_own, e_out, e_in, c_in, b_red, e_red,
     c_out, c_all, d_out, d_all,
-    load_sem, sems,
+    turns, coef, load_sem, sems,
 ):
     s = lax.axis_index("strip")
     me = lax.axis_index("cross")
@@ -52,12 +53,15 @@
         )
         for j in range(blocks)
     ]
+    turn_loads = [
+        pltpu.make_async_copy(ref, turns.at[j], load_sem.at[5 + blocks + j])
+        for j, ref in enumerate((phase_fwd, gain_fwd, phase_back, gain_back))
+    ]
     loads[0].start()
     loads[1].start()
     for copy in inv_loads:
         copy.start()
-    for copy in loads[2:]:
-        copy.start()
+    loads[2].start()
 
     barrier = pltpu.get_barrier_semaphore()
 
@@ -125,12 +129,6 @@
     def share_sent(kind, buf):
         others(lambda peer: remote(kind, buf.at[me], buf.at[me], s, peer).wait_send())
 
-    def pass_on(kind, src, buf, strip):
-        everyone(lambda peer: remote(kind, src, buf.at[me], strip, peer).start())
-
-    def passed_on(kind, src, buf, strip):
-        everyone(lambda peer: remote(kind, src, buf.at[me], strip, peer).wait_send())
-
     def split(value, own, out):
         part = value.shape[0] // n
         for k in range(n):
@@ -141,43 +139,62 @@
     def joined(buf):
         return jnp.concatenate([buf[k] for k in range(n)], axis=0)
 
-    def rotated(value, phase, gain):
+    def rotated(value, at):
         real, imag = value[:, :half], value[:, half:]
-        cosine, sine, g = jnp.cos(phase[...]), jnp.sin(phase[...]), gain[...]
+        cosine, sine = coef[at], coef[at + 1]
         return jnp.concatenate(
-            [g * (cosine * real - sine * imag), g * (sine * real + cosine * imag)], axis=1
+            [cosine * real - sine * imag, sine * real + cosine * imag], axis=1
         )
 
     loads[0].wait()
     loads[1].wait()
-    for j in range(blocks):
-        inv_loads[j].wait()
-        product = dot(x_f[...], inv[j])
-        p[:, j * width:(j + 1) * width] = product[:angles]
-        u_f[:, j * width:(j + 1) * width] = product[angles:].astype(BF)
+
+    @pl.when(is_first)
+    def _():
+        for j in range(blocks):
+            inv_loads[j].wait()
+            p[:, j * width:(j + 1) * width] = dot(x_f[:angles], inv[j])
+
+    @pl.when(s > 0)
+    def _():
+        for j in range(blocks):
+            inv_loads[j].wait()
+            product = dot(x_f[...], inv[j])
+            p[:, j * width:(j + 1) * width] = product[:angles]
+            u_f[:, j * width:(j + 1) * width] = product[angles:].astype(BF)
+
+    for copy in loads[3:] + turn_loads:
+        copy.start()
     loads[2].wait()
 
     @pl.when(inner)
     def _():
         split(dot(u_f[...], agg_f[...]), t_own, t_out)
 
-    @pl.when(s < strips - 1)
+    @pl.when(is_first)
     def _():
         split(dot(p[...].astype(BF), agg_f[...]), b_own, b_out)
 
     greeted = (n - 1) + jnp.where(s > 0, n, 0) + jnp.where(s < strips - 1, n, 0)
     pl.semaphore_wait(barrier, greeted)
 
-    @pl.when(s < strips - 1)
-    def _():
+    @pl.when(is_first)
+    def _():
+        everyone(lambda peer: remote(C_IN, b_out.at[peer], c_in.at[me], s + 1, peer).start())
+
+    @pl.when(inner)
+    def _():
+        scatter(T_RS, t_out, t_in)
+        split(dot(p[...].astype(BF), agg_f[...]), b_own, b_out)
         scatter(B_RS, b_out, b_in)
-
-    @pl.when(inner)
-    def _():
-        scatter(T_RS, t_out, t_in)
 
     loads[3].wait()
     loads[4].wait()
+    for copy in turn_loads:
+        copy.wait()
+    for at in (0, 2):
+        coef[at] = jnp.cos(turns[at]) * turns[at + 1]
+        coef[at + 1] = jnp.sin(turns[at]) * turns[at + 1]
 
     @pl.when(is_last)
     def _():
@@ -194,33 +211,39 @@
     def _():
         split(dot(u_b[...], agg_b[...]), n_own, n_out)
 
-    @pl.when(s < strips - 1)
-    def _():
-        b_red[...] = total(B_RS, b_own, b_in)
-
-    @pl.when(is_first)
-    def _():
-        c_out[...] = b_red[...].astype(BF)
-        pass_on(C_ON, c_out, c_all, s + 1)
-
     @pl.when(inner)
     def _():
         t_all[me] = total(T_RS, t_own, t_in).astype(BF)
         share(T_AG, t_all)
+        b_red[...] = total(B_RS, b_own, b_in)
 
     @pl.when(s > 0)
     def _():
         scatter(N_RS, n_out, n_in)
 
+    def take_carry():
+        @pl.when(s == 1)
+        def _():
+            everyone(lambda peer: arrived(C_IN, c_in, peer))
+            value = c_in[0].astype(F32)
+            for j in range(1, n):
+                value = value + c_in[j].astype(F32)
+            c_all[me] = value.astype(BF)
+
+        @pl.when(s > 1)
+        def _():
+            arrived(C_ON, c_all, me)
+
     @pl.when(inner)
     def _():
         others(lambda peer: arrived(T_AG, t_all, peer))
-        arrived(C_ON, c_all, me)
+        matrix = joined(t_all)
+        take_carry()
         held = c_all[me]
-        leaving = rotated(held.astype(F32), phase_fwd, gain_fwd) + b_red[...]
-        leaving = leaving - dot(held, joined(t_all))
-        c_out[...] = leaving.astype(BF)
-        pass_on(C_ON, c_out, c_all, s + 1)
+        leaving = rotated(held.astype(F32), 0) + b_red[...]
+        c_out[...] = (leaving - dot(held, matrix)).astype(BF)
+        remote(C_ON, c_out, c_all.at[me], s + 1, me).start()
+        share(C_SH, c_all)
 
     @pl.when(s > 0)
     def _():
@@ -231,9 +254,23 @@
     def _():
         e_red[...] = total(E_RS, e_own, e_in)
         others(lambda peer: arrived(N_AG, n_all, peer))
-        arrived(C_ON, c_all, me)
-        d_out[...] = (e_red[...] - dot(c_all[me], joined(n_all))).astype(BF)
-        pass_on(D_ON, d_out, d_all, s - 1)
+        matrix = joined(n_all)
+        take_carry()
+        d_out[...] = (e_red[...] - dot(c_all[me], matrix)).astype(BF)
+
+    def send_back():
+        @pl.when(s == 1)
+        def _():
+            everyone(lambda peer: remote(D_ON, d_out, d_all.at[me], s - 1, peer).start())
+
+        @pl.when(s > 1)
+        def _():
+            remote(D_ON, d_out, d_all.at[me], s - 1, me).start()
+
+    @pl.when(is_last)
+    def _():
+        send_back()
+        share(C_SH, c_all)
 
     @pl.when(is_first)
     def _():
@@ -241,7 +278,7 @@
 
     @pl.when(s > 0)
     def _():
-        others(lambda peer: arrived(C_ON, c_all, peer))
+        others(lambda peer: arrived(C_SH, c_all, peer))
         first_ref[0] = p[...] - dot(joined(c_all), u_f[...])
 
     @pl.when(inner)
@@ -250,12 +287,13 @@
         scatter(E_RS, e_out, e_in)
         others(lambda peer: arrived(N_AG, n_all, peer))
         e_red[...] = total(E_RS, e_own, e_in)
+        matrix = joined(n_all)
         arrived(D_ON, d_all, me)
         held = d_all[me]
-        leaving = rotated(held.astype(F32), phase_back, gain_back) + e_red[...]
-        leaving = leaving - dot(held, joined(n_all))
-        d_out[...] = leaving.astype(BF)
-        pass_on(D_ON, d_out, d_all, s - 1)
+        leaving = rotated(held.astype(F32), 2) + e_red[...]
+        d_out[...] = (leaving - dot(held, matrix)).astype(BF)
+        send_back()
+        share(D_SH, d_all)
 
     @pl.when(is_last)
     def _():
@@ -263,29 +301,42 @@
 
     @pl.when(is_first)
     def _():
-        arrived(D_ON, d_all, me)
+        everyone(lambda peer: arrived(D_ON, d_all, peer))
+
+    @pl.when(inner)
+    def _():
+        others(lambda peer: arrived(D_SH, d_all, peer))
 
     @pl.when(s < strips - 1)
     def _():
-        others(lambda peer: arrived(D_ON, d_all, peer))
         second_ref[0] = first_ref[0] - dot(joined(d_all), u_b[...])
+
+    @pl.when(is_first)
+    def _():
+        everyone(lambda peer: remote(C_IN, b_out.at[peer], c_in.at[me], s + 1, peer).wait_send())
 
     @pl.when(inner)
     def _():
         scatter_sent(T_RS, t_out, t_in)
         share_sent(T_AG, t_all)
-
-    @pl.when(s < strips - 1)
-    def _():
         scatter_sent(B_RS, b_out, b_in)
-        passed_on(C_ON, c_out, c_all, s + 1)
-
-    @pl.when(s > 0)
-    def _():
+        remote(C_ON, c_out, c_all.at[me], s + 1, me).wait_send()
+        share_sent(D_SH, d_all)
+
+    @pl.when(s > 0)
+    def _():
+        share_sent(C_SH, c_all)
         scatter_sent(N_RS, n_out, n_in)
         share_sent(N_AG, n_all)
         scatter_sent(E_RS, e_out, e_in)
-        passed_on(D_ON, d_out, d_all, s - 1)
+
+    @pl.when(s == 1)
+    def _():
+        everyone(lambda peer: remote(D_ON, d_out, d_all.at[me], s - 1, peer).wait_send())
+
+    @pl.when(s > 1)
+    def _():
+        remote(D_ON, d_out, d_all.at[me], s - 1, me).wait_send()
 
 
 def body(strips, n, rhs, inverse, dis_fwd, agg_fwd, phase_fwd, gain_fwd, dis_back, agg_back, phase_back, gain_back):
@@ -296,11 +347,11 @@
     rows, part = angles // n, modes // n
     hbm = pl.BlockSpec(memory_space=pl.ANY)
     vmem = pl.BlockSpec(memory_space=pltpu.VMEM)
-    out = jax.ShapeDtypeStruct((1, angles, unk), F32)
+    out = pltpu.VMEM((1, angles, unk), F32)
     return pl.pallas_call(
         functools.partial(kernel, strips, n, width),
         out_shape=(out, out),
-        in_specs=[hbm, hbm, hbm, hbm, vmem, vmem, hbm, hbm, vmem, vmem],
+        in_specs=[hbm] * 10,
         out_specs=(vmem, vmem),
         scratch_shapes=[
             pltpu.VMEM((angles + modes, unk), BF),
@@ -313,10 +364,11 @@
             pltpu.VMEM((modes, unk), BF),
         ]
         + [pltpu.VMEM((n, part, modes), kind) for kind in (F32, BF, BF) * 2 + (BF, BF)]
-        + [pltpu.VMEM((n, rows, modes), kind) for kind in (F32, BF, BF) * 2]
+        + [pltpu.VMEM((n, rows, modes), kind) for kind in (F32, BF, BF) * 2 + (BF,)]
         + [pltpu.VMEM((rows, modes), F32)] * 2
         + [pltpu.VMEM((rows, modes), BF), pltpu.VMEM((n, rows, modes), BF)] * 2
-        + [pltpu.SemaphoreType.DMA((5 + blocks,)), pltpu.SemaphoreType.DMA((8, 2, n))],
+        + [pltpu.VMEM((4, 1, modes // 2), F32)] * 2
+        + [pltpu.SemaphoreType.DMA((9 + blocks,)), pltpu.SemaphoreType.DMA((KINDS, 2, n))],
         compiler_params=pltpu.CompilerParams(
             collective_id=0, has_side_effects=True, vmem_limit_bytes=60 * 1024 * 1024
         ),

time: 40.2 us -> 38 us (0.945)
  local copies, waits for them, and re-layouts: 3.63 us -> 1.54 us
    unnamed x2, local copies, waits for them, and re-layouts: 3.63 us -> 1.54 us
where the time goes in v2:
time: 38 us; the launch traced here: 37.8 us
  Pallas kernels  35.6 us (94%)
  local copies, waits for them, and re-layouts  1.54 us (4%)
  between operations  0.64 us (2%)
    pallas_call x1, Pallas kernels, body(): pl.pallas_call(functools.partial(kernel, strips, n, width), out_shape=(ou...  35.6 us
    unnamed x2, local copies, waits for them, and re-layouts  1.54 us

profile of v2, /device:TPU:0, one launch (start us, length us, event | category | flops | bytes accessed | tf_op | source)
XLA Modules:
  0.0 37.8 jit_solution(12048465996513205134)
XLA Ops:
  0.6 35.6 %shard_map.113 = (f32[1,64,1792]{2,1,0:T(8,128)S(1)}, f32[1,64,1792]{2,1,0:T(8,128)S(1)}) custom-call(bf16[1,64,1792]{2,1,0:T(8,128)(2,1)} %rhs.1, bf16[1,1,1792,1792]{3,2,1,0:T(8,128)(2,1)} %inverse.1, bf16[1,1,256,1792]{3,2,1,0:T(8,128)(2,1)} %dis_fwd.1, bf16[1,1792,256]{2,1,0:T(8,128)(2,1)} %agg_fwd.1, f32[1,128]{1,0:T(1,128)} %phase_fwd.1, ...), custom_call_target="tpu_custom_call" | custom-call | tf_op jit(solution)/shard_map/pallas_call | solution.py:351
  36.3 0.8 %copy.14 = f32[1,64,1792]{2,1,0:T(8,128)} copy(f32[1,64,1792]{2,1,0:T(8,128)S(1)} %get-tuple-element.2) | data formatting | bytes 917504
  37.0 0.8 %copy.15 = f32[1,64,1792]{2,1,0:T(8,128)} copy(f32[1,64,1792]{2,1,0:T(8,128)S(1)} %get-tuple-element.3) | data formatting | bytes 917504

commit v3 on v2

--- a/solution.py
+++ b/solution.py
@@ -40,13 +40,14 @@
     blocks = unk // width
     rows = angles // n
 
-    loads = [
-        pltpu.make_async_copy(rhs.at[0], x_f.at[pl.ds(0, angles)], load_sem.at[0]),
-        pltpu.make_async_copy(dis_fwd.at[0, 0], x_f.at[pl.ds(angles, modes)], load_sem.at[1]),
-        pltpu.make_async_copy(agg_fwd.at[0], agg_f, load_sem.at[2]),
-        pltpu.make_async_copy(dis_back.at[0, 0], x_b, load_sem.at[3]),
-        pltpu.make_async_copy(agg_back.at[0], agg_b, load_sem.at[4]),
-    ]
+    load_rhs = pltpu.make_async_copy(rhs.at[0], x_b.at[pl.ds(0, angles)], load_sem.at[0])
+    load_dis = pltpu.make_async_copy(dis_fwd.at[0, 0], x_f, load_sem.at[1])
+    load_agg = pltpu.make_async_copy(agg_fwd.at[0], agg_f, load_sem.at[2])
+    load_last = pltpu.make_async_copy(agg_back.at[0], agg_f, load_sem.at[2])
+    load_dis_b = pltpu.make_async_copy(
+        dis_back.at[0, 0], x_b.at[pl.ds(angles, modes)], load_sem.at[3]
+    )
+    load_agg_b = pltpu.make_async_copy(agg_back.at[0], agg_b, load_sem.at[4])
     inv_loads = [
         pltpu.make_async_copy(
             inverse.at[0, 0, :, pl.ds(j * width, width)], inv.at[j], load_sem.at[5 + j]
@@ -57,11 +58,39 @@
         pltpu.make_async_copy(ref, turns.at[j], load_sem.at[5 + blocks + j])
         for j, ref in enumerate((phase_fwd, gain_fwd, phase_back, gain_back))
     ]
-    loads[0].start()
-    loads[1].start()
+    @pl.when(is_first)
+    def _():
+        load_rhs.start()
+
+    @pl.when(s > 0)
+    def _():
+        load_dis.start()
+
+    @pl.when(is_last)
+    def _():
+        load_last.start()
+
+    @pl.when(s < strips - 1)
+    def _():
+        load_agg.start()
+
     for copy in inv_loads:
         copy.start()
-    loads[2].start()
+
+    @pl.when(s > 0)
+    def _():
+        load_rhs.start()
+
+    @pl.when(s < strips - 1)
+    def _():
+        load_dis_b.start()
+
+    @pl.when(inner)
+    def _():
+        load_agg_b.start()
+
+    for copy in turn_loads:
+        copy.start()
 
     barrier = pltpu.get_barrier_semaphore()
 
@@ -146,34 +175,36 @@
             [cosine * real - sine * imag, sine * real + cosine * imag], axis=1
         )
 
-    loads[0].wait()
-    loads[1].wait()
-
-    @pl.when(is_first)
-    def _():
+    def columns(j):
+        return slice(j * width, (j + 1) * width)
+
+    load_agg.wait()
+
+    @pl.when(is_first)
+    def _():
+        load_rhs.wait()
+        value = None
         for j in range(blocks):
             inv_loads[j].wait()
-            p[:, j * width:(j + 1) * width] = dot(x_f[:angles], inv[j])
-
-    @pl.when(s > 0)
-    def _():
+            product = dot(x_b[:angles], inv[j])
+            p[:, columns(j)] = product
+            term = dot(product.astype(BF), agg_f[columns(j)])
+            value = term if value is None else value + term
+        split(value, b_own, b_out)
+
+    @pl.when(s > 0)
+    def _():
+        load_dis.wait()
         for j in range(blocks):
             inv_loads[j].wait()
-            product = dot(x_f[...], inv[j])
-            p[:, j * width:(j + 1) * width] = product[:angles]
-            u_f[:, j * width:(j + 1) * width] = product[angles:].astype(BF)
-
-    for copy in loads[3:] + turn_loads:
-        copy.start()
-    loads[2].wait()
-
-    @pl.when(inner)
-    def _():
-        split(dot(u_f[...], agg_f[...]), t_own, t_out)
-
-    @pl.when(is_first)
-    def _():
-        split(dot(p[...].astype(BF), agg_f[...]), b_own, b_out)
+            product = dot(x_f[...], inv[j]).astype(BF)
+            u_f[:, columns(j)] = product
+            term = dot(product, agg_f[columns(j)]).reshape(t_own.shape)
+            if j == 0:
+                t_own[...] = term
+            else:
+                t_own[...] += term
+        t_out[...] = t_own[...].astype(BF)
 
     greeted = (n - 1) + jnp.where(s > 0, n, 0) + jnp.where(s < strips - 1, n, 0)
     pl.semaphore_wait(barrier, greeted)
@@ -182,42 +213,52 @@
     def _():
         everyone(lambda peer: remote(C_IN, b_out.at[peer], c_in.at[me], s + 1, peer).start())
 
-    @pl.when(inner)
+    @pl.when(s > 0)
     def _():
         scatter(T_RS, t_out, t_in)
-        split(dot(p[...].astype(BF), agg_f[...]), b_own, b_out)
+        load_rhs.wait()
+        value = None
+        for j in range(blocks):
+            product = dot(x_b[:angles], inv[j])
+            p[:, columns(j)] = product
+            term = dot(product.astype(BF), agg_f[columns(j)])
+            value = term if value is None else value + term
+        split(value, b_own, b_out)
         scatter(B_RS, b_out, b_in)
 
-    loads[3].wait()
-    loads[4].wait()
     for copy in turn_loads:
         copy.wait()
     for at in (0, 2):
         coef[at] = jnp.cos(turns[at]) * turns[at + 1]
         coef[at + 1] = jnp.sin(turns[at]) * turns[at + 1]
 
-    @pl.when(is_last)
-    def _():
-        split(dot(p[...].astype(BF), agg_b[...]), e_own, e_out)
-        scatter(E_RS, e_out, e_in)
-        split(dot(u_f[...], agg_b[...]), n_own, n_out)
-
-    @pl.when(s < strips - 1)
-    def _():
+    @pl.when(is_first)
+    def _():
+        load_dis_b.wait()
         for j in range(blocks):
-            u_b[:, j * width:(j + 1) * width] = dot(x_b[...], inv[j]).astype(BF)
-
-    @pl.when(inner)
-    def _():
-        split(dot(u_b[...], agg_b[...]), n_own, n_out)
-
-    @pl.when(inner)
+            u_b[:, columns(j)] = dot(x_b[angles:], inv[j]).astype(BF)
+
+    @pl.when(inner)
+    def _():
+        load_dis_b.wait()
+        load_agg_b.wait()
+        for j in range(blocks):
+            product = dot(x_b[angles:], inv[j]).astype(BF)
+            u_b[:, columns(j)] = product
+            term = dot(product, agg_b[columns(j)]).reshape(n_own.shape)
+            if j == 0:
+                n_own[...] = term
+            else:
+                n_own[...] += term
+        n_out[...] = n_own[...].astype(BF)
+
+    @pl.when(s > 0)
     def _():
         t_all[me] = total(T_RS, t_own, t_in).astype(BF)
         share(T_AG, t_all)
         b_red[...] = total(B_RS, b_own, b_in)
 
-    @pl.when(s > 0)
+    @pl.when(inner)
     def _():
         scatter(N_RS, n_out, n_in)
 
@@ -245,18 +286,17 @@
         remote(C_ON, c_out, c_all.at[me], s + 1, me).start()
         share(C_SH, c_all)
 
-    @pl.when(s > 0)
+    @pl.when(inner)
     def _():
         n_all[me] = total(N_RS, n_own, n_in).astype(BF)
         share(N_AG, n_all)
 
     @pl.when(is_last)
     def _():
-        e_red[...] = total(E_RS, e_own, e_in)
-        others(lambda peer: arrived(N_AG, n_all, peer))
-        matrix = joined(n_all)
+        others(lambda peer: arrived(T_AG, t_all, peer))
+        matrix = joined(t_all)
         take_carry()
-        d_out[...] = (e_red[...] - dot(c_all[me], matrix)).astype(BF)
+        d_out[...] = (b_red[...] - dot(c_all[me], matrix)).astype(BF)
 
     def send_back():
         @pl.when(s == 1)
@@ -317,18 +357,18 @@
 
     @pl.when(inner)
     def _():
+        scatter_sent(N_RS, n_out, n_in)
+        share_sent(N_AG, n_all)
+        scatter_sent(E_RS, e_out, e_in)
+        remote(C_ON, c_out, c_all.at[me], s + 1, me).wait_send()
+        share_sent(D_SH, d_all)
+
+    @pl.when(s > 0)
+    def _():
         scatter_sent(T_RS, t_out, t_in)
         share_sent(T_AG, t_all)
         scatter_sent(B_RS, b_out, b_in)
-        remote(C_ON, c_out, c_all.at[me], s + 1, me).wait_send()
-        share_sent(D_SH, d_all)
-
-    @pl.when(s > 0)
-    def _():
         share_sent(C_SH, c_all)
-        scatter_sent(N_RS, n_out, n_in)
-        share_sent(N_AG, n_all)
-        scatter_sent(E_RS, e_out, e_in)
 
     @pl.when(s == 1)
     def _():
@@ -354,8 +394,8 @@
         in_specs=[hbm] * 10,
         out_specs=(vmem, vmem),
         scratch_shapes=[
+            pltpu.VMEM((modes, unk), BF),
             pltpu.VMEM((angles + modes, unk), BF),
-            pltpu.VMEM((modes, unk), BF),
             pltpu.VMEM((blocks, unk, width), BF),
             pltpu.VMEM((unk, modes), BF),
             pltpu.VMEM((unk, modes), BF),

time: 38 us -> 38 us (level)
  no operation moved by 1% of the time
where the time goes in v3:
time: 38 us; the launch traced here: 37.9 us
  Pallas kernels  35.7 us (94%)
  local copies, waits for them, and re-layouts  1.54 us (4%)
  between operations  0.64 us (2%)
    pallas_call x1, Pallas kernels, body(): pl.pallas_call(functools.partial(kernel, strips, n, width), out_shape=(ou...  35.7 us
    unnamed x2, local copies, waits for them, and re-layouts  1.54 us

profile of v3, /device:TPU:0, one launch (start us, length us, event | category | flops | bytes accessed | tf_op | source)
XLA Modules:
  0.0 37.9 jit_solution(9280161553637780415)
XLA Ops:
  0.6 35.7 %shard_map.113 = (f32[1,64,1792]{2,1,0:T(8,128)S(1)}, f32[1,64,1792]{2,1,0:T(8,128)S(1)}) custom-call(bf16[1,64,1792]{2,1,0:T(8,128)(2,1)} %rhs.1, bf16[1,1,1792,1792]{3,2,1,0:T(8,128)(2,1)} %inverse.1, bf16[1,1,256,1792]{3,2,1,0:T(8,128)(2,1)} %dis_fwd.1, bf16[1,1792,256]{2,1,0:T(8,128)(2,1)} %agg_fwd.1, f32[1,128]{1,0:T(1,128)} %phase_fwd.1, ...), custom_call_target="tpu_custom_call" | custom-call | tf_op jit(solution)/shard_map/pallas_call | solution.py:391
  36.3 0.8 %copy.14 = f32[1,64,1792]{2,1,0:T(8,128)} copy(f32[1,64,1792]{2,1,0:T(8,128)S(1)} %get-tuple-element.2) | data formatting | bytes 917504
  37.1 0.8 %copy.15 = f32[1,64,1792]{2,1,0:T(8,128)} copy(f32[1,64,1792]{2,1,0:T(8,128)S(1)} %get-tuple-element.3) | data formatting | bytes 917504

commit v4 on v3

--- a/solution.py
+++ b/solution.py
@@ -238,6 +238,11 @@
         for j in range(blocks):
             u_b[:, columns(j)] = dot(x_b[angles:], inv[j]).astype(BF)
 
+    @pl.when(s > 0)
+    def _():
+        t_all[me] = total(T_RS, t_own, t_in).astype(BF)
+        share(T_AG, t_all)
+
     @pl.when(inner)
     def _():
         load_dis_b.wait()
@@ -254,8 +259,6 @@
 
     @pl.when(s > 0)
     def _():
-        t_all[me] = total(T_RS, t_own, t_in).astype(BF)
-        share(T_AG, t_all)
         b_red[...] = total(B_RS, b_own, b_in)
 
     @pl.when(inner)

time: 38 us -> 36.9 us (0.971)
  Pallas kernels: 35.7 us -> 34.6 us
    pallas_call x1, Pallas kernels: 35.7 us -> 34.6 us  [body(): pl.pallas_call(functools.partial(kernel, strips, n, width), out_shape=(ou...]
where the time goes in v4:
time: 36.9 us; the launch traced here: 36.8 us
  Pallas kernels  34.6 us (94%)
  local copies, waits for them, and re-layouts  1.54 us (4%)
  between operations  0.64 us (2%)
    pallas_call x1, Pallas kernels, body(): pl.pallas_call(functools.partial(kernel, strips, n, width), out_shape=(ou...  34.6 us
    unnamed x2, local copies, waits for them, and re-layouts  1.54 us

profile of v4, /device:TPU:0, one launch (start us, length us, event | category | flops | bytes accessed | tf_op | source)
XLA Modules:
  0.0 36.8 jit_solution(3304614114125858924)
XLA Ops:
  0.6 34.6 %shard_map.113 = (f32[1,64,1792]{2,1,0:T(8,128)S(1)}, f32[1,64,1792]{2,1,0:T(8,128)S(1)}) custom-call(bf16[1,64,1792]{2,1,0:T(8,128)(2,1)} %rhs.1, bf16[1,1,1792,1792]{3,2,1,0:T(8,128)(2,1)} %inverse.1, bf16[1,1,256,1792]{3,2,1,0:T(8,128)(2,1)} %dis_fwd.1, bf16[1,1792,256]{2,1,0:T(8,128)(2,1)} %agg_fwd.1, f32[1,128]{1,0:T(1,128)} %phase_fwd.1, ...), custom_call_target="tpu_custom_call" | custom-call | tf_op jit(solution)/shard_map/pallas_call | solution.py:394
  35.2 0.8 %copy.14 = f32[1,64,1792]{2,1,0:T(8,128)} copy(f32[1,64,1792]{2,1,0:T(8,128)S(1)} %get-tuple-element.2) | data formatting | bytes 917504
  36.0 0.8 %copy.15 = f32[1,64,1792]{2,1,0:T(8,128)} copy(f32[1,64,1792]{2,1,0:T(8,128)S(1)} %get-tuple-element.3) | data formatting | bytes 917504
